TPU v7x, 32 devices: a whole 2x2x4 slice. The times are simulated.
32 devices in a mesh: surf: 8 (over y, x, core), norm: 4 (over z).
Axes of the slice: x: 2, y: 2, z: 4, core: 2. Of those that a mesh axis runs over, the one named last changes fastest.
Arguments:
- mode_shapes: bfloat16 [128, 64, 3, 256], P('surf'), may hold values from -6 to 6
- amplitude: float32 [128], replicated, may hold values from -0.046875 to 0.046875
- mode_patch: int32 [128], replicated, may hold values from 0 to 3
- column_patch: int32 [64, 256], replicated, may hold values from 0 to 3
- wall_mask: int32 [64, 256], P('surf'), may hold values 0 or 1
- offsets: int32 [64, 256], P('surf'), may hold values from 0 to 127
- coupling: float32 [64, 64, 256], P('norm', 'surf'), may hold values from 0.5 to 2
- pivot_inv: float32 [64, 64, 9, 256], P('norm', 'surf'), may hold values from -2 to 2
- stiffness: float32 [64, 64, 256], P('norm', 'surf'), may hold values from 0.00021972656 to 0.0005126953
Outputs:
- displacement: float32 [64, 64, 3, 256], P('norm', 'surf')
All inputs are finite; a program needn't handle non-finite values. No bound on the sum of `wall_mask` on one device may be relied on, other than what follows from the above.
Results may differ from a plain program's by a relative error of at most 0.0006.
Values may be sent and summed in bfloat16 or wider, within the bound.
A program may use at most 64 MiB of HBM per device.

v0:
```python
import jax
import jax.numpy as jnp
from jax import lax
from jax.sharding import PartitionSpec as P

SWEEPS = 3


def shifted(shard, axis, by):
    count = lax.axis_size(axis)
    pairs = [(i, i + by) for i in range(count) if 0 <= i + by < count]
    return lax.ppermute(shard, axis, pairs)


def shortened(shard):

    def short(part):
        return part.astype(jnp.bfloat16) if part.dtype == jnp.float32 else part

    return jax.tree.map(short, shard)


def padded_2(block, sides, width):
    for axis, dim in sides:
        count = lax.axis_size(axis)
        forward = [(i, i + 1) for i in range(count - 1)]
        forward.append((count - 1, 0))
        backward = [(target, source) for source, target in forward]
        low = lax.ppermute(
            lax.slice_in_dim(block, block.shape[dim] - width, None, axis=dim), axis, forward
        )
        high = lax.ppermute(lax.slice_in_dim(block, 0, width, axis=dim), axis, backward)
        block = jnp.concatenate([low, block, high], axis=dim)
    return block


def carried_in(part, axis, combine, identity, reverse):
    count = lax.axis_size(axis)
    place = lax.axis_index(axis)
    ahead = count - 1 - place if reverse else place
    gathered = jax.tree.map(lambda a: lax.all_gather(a, axis), part)
    state = jax.tree.map(lambda a, e: jnp.zeros_like(a) + jnp.asarray(e, a.dtype), part, identity)

    def one(hop, state):
        source = count - 1 - hop if reverse else hop
        return combine(
            state, jax.tree.map(lambda a: lax.dynamic_index_in_dim(a, source, 0, False), gathered)
        )

    return lax.fori_loop(0, ahead, one, state)


def mat_vec(matrix, vector):
    blocks = matrix.reshape(matrix.shape[:-2] + (3, 3, matrix.shape[-1]))
    return jnp.sum(blocks * vector[..., None, :, :], axis=-2)


def mat_mat(left_matrix, right_matrix):
    line_width = left_matrix.shape[-1]
    left_blocks = left_matrix.reshape(left_matrix.shape[:-2] + (3, 3, line_width))
    right_blocks = right_matrix.reshape(right_matrix.shape[:-2] + (3, 3, line_width))
    product = jnp.sum(left_blocks[..., :, :, None, :] * right_blocks[..., None, :, :, :], axis=-3)
    return product.reshape(left_matrix.shape)


def compose(earlier, later):
    earlier_map, earlier_shift = earlier
    later_map, later_shift = later
    return (mat_mat(later_map, earlier_map), mat_vec(later_map, earlier_shift) + later_shift)


def forward(pivots, lower_link, right_side, inflow):
    state_now = inflow
    results = []
    for cell in range(pivots.shape[0]):
        state_now = mat_vec(
            pivots[cell], right_side[cell] + lower_link[cell][:, None, :] * state_now
        )
        results.append(state_now)
    return (jnp.stack(results, axis=0), state_now)


def backward(pivots, upper_link, forward_values, outflow):
    state_now = outflow
    results = []
    for cell in range(pivots.shape[0] - 1, -1, -1):
        state_now = forward_values[cell] + mat_vec(
            pivots[cell], upper_link[cell][:, None, :] * state_now
        )
        results.append(state_now)
    return (jnp.stack(results[::-1], axis=0), state_now)


def prefix_maps(pivots, links, identity_map, backwards):
    state_now = identity_map
    results = []
    cell_total = pivots.shape[0]
    order = range(cell_total - 1, -1, -1) if backwards else range(cell_total)
    for cell in order:
        state_now = mat_mat(pivots[cell] * links[cell][:, None, :], state_now)
        results.append(state_now)
    if backwards:
        results = results[::-1]
    return jnp.stack(results, axis=0)


def neighbours(padded):
    centre = padded[:, 1:-1]
    zero_column = jnp.zeros_like(centre[..., :1])
    neighbour_sum = padded[:, 2:] + padded[:, :-2]
    neighbour_sum = neighbour_sum + jnp.concatenate([centre[..., 1:], zero_column], axis=-1)
    return neighbour_sum + jnp.concatenate([zero_column, centre[..., :-1]], axis=-1)


def per_device(
    mode_shapes,
    amplitude,
    mode_patch,
    column_patch,
    wall_mask,
    offsets,
    coupling,
    pivot_inv,
    stiffness,
):
    row_count = wall_mask.shape[0]
    line_width = wall_mask.shape[1]
    cell_count = coupling.shape[0]
    chain_size = lax.axis_size("norm")
    position = lax.axis_index("norm")
    blocks = lax.all_to_all(mode_shapes, "surf", split_axis=1, concat_axis=0, tiled=True)
    own_patch = lax.dynamic_slice_in_dim(
        column_patch, lax.axis_index("surf") * row_count, row_count, 0
    )
    weights = amplitude[:, None, None] * (mode_patch[:, None, None] == own_patch[None]).astype(
        jnp.float32
    )
    wall_shift = jnp.sum(weights[:, :, None, :] * blocks.astype(jnp.float32), axis=0)
    wall_shift = wall_shift * wall_mask[:, None, :].astype(jnp.float32)
    depth_index = position * cell_count + jnp.arange(cell_count, dtype=jnp.int32)
    lower_link = jnp.where(
        depth_index[:, None, None] == offsets[None], jnp.zeros_like(coupling), coupling
    )
    next_row = shifted(lower_link[0], "norm", -1)
    upper_link = jnp.concatenate([lower_link[1:], next_row[None]], axis=0)
    blend_weight = 1.0 - depth_index.astype(jnp.float32) / (cell_count * chain_size)
    displaced = blend_weight[:, None, None, None] * wall_shift[None]
    wall_term = jnp.where(
        position == 0, lower_link[0][:, None, :] * wall_shift, jnp.zeros_like(wall_shift)
    )
    identity_map = jnp.eye(3, dtype=jnp.float32).reshape(9)[None, :, None] * jnp.ones(
        (row_count, 1, line_width), jnp.float32
    )
    zero_state = jnp.zeros((row_count, 3, line_width), jnp.float32)
    lower_prefix = prefix_maps(pivot_inv, lower_link, identity_map, False)
    upper_prefix = prefix_maps(pivot_inv, upper_link, identity_map, True)
    lower_map = lower_prefix[-1]
    upper_map = upper_prefix[0]
    for sweep_index in range(SWEEPS):
        padded = padded_2(shortened(displaced), (("surf", 1),), 1).astype(displaced.dtype)
        right_side = stiffness[:, :, None, :] * neighbours(padded)
        right_side = right_side.at[0].add(wall_term)
        local_values, segment_end = forward(pivot_inv, lower_link, right_side, zero_state)
        inflow = carried_in(
            (lower_map, segment_end), "norm", compose, (identity_map, zero_state), False
        )[1]
        forward_values = local_values + mat_vec(lower_prefix, inflow[None])
        local_solved, segment_top = backward(pivot_inv, upper_link, forward_values, zero_state)
        outflow = carried_in(
            (upper_map, segment_top), "norm", compose, (identity_map, zero_state), True
        )[1]
        displaced = local_solved + mat_vec(upper_prefix, outflow[None])
    return displaced


def solution(mesh):
    return jax.shard_map(
        per_device,
        mesh=mesh,
        in_specs=(
            P("surf", None, None, None),
            P(),
            P(),
            P(),
            P("surf", None),
            P("surf", None),
            P("norm", "surf", None),
            P("norm", "surf", None, None),
            P("norm", "surf", None),
        ),
        out_specs=P("norm", "surf", None, None),
        check_vma=False,
    )
```

profile of v0, /device:TPU:0, one launch (start us, length us, event | category | flops | bytes accessed | tf_op | source)
XLA Modules:
  0.0 240.2 jit_solution(8377368849300692024)
XLA Ops:
  0.0 3.5 %copy.1008 = bf16[16,64,3,256]{3,0,2,1:T(8,128)(2,1)} copy(bf16[16,64,3,256]{3,1,2,0:T(8,128)(2,1)} %param.27) | data formatting | bytes 3145728 | tf_op args[0]
  3.5 5.3 %all-to-all-start = ((bf16[16,64,3,256]{3,0,2,1:T(8,128)(2,1)}), bf16[16,64,3,256]{3,0,2,1:T(8,128)(2,1)S(1)}, u32[]{:S(2)}, u32[]{:S(2)}) async-start(bf16[16,64,3,256]{3,0,2,1:T(8,128)(2,1)} %copy.1008), calls=%async_computation | async-start | bytes 3145728 | tf_op jit(solution)/shard_map/all_to_all | solution.py:131
  13.7 2.1 fusion.110
  15.9 14.0 %all-to-all-done = bf16[16,64,3,256]{3,0,2,1:T(8,128)(2,1)S(1)} async-done(((bf16[16,64,3,256]{3,0,2,1:T(8,128)(2,1)}), bf16[16,64,3,256]{3,0,2,1:T(8,128)(2,1)S(1)}, u32[]{:S(2)}, u32[]{:S(2)}) %all-to-all-start) | async-done | bytes 1572896 | tf_op jit(solution)/shard_map/all_to_all | solution.py:131
  30.3 3.9 %fusion = f32[8,3,256]{2,1,0:T(4,128)S(1)} fusion(f32[16,8,8,3,256]{4,0,3,2,1:T(8,128)S(1)} %bitcast_convert_fusion, f32[8,16,8,256]{3,1,2,0:T(8,128)S(1)} %compare_select_fusion), kind=kLoop, calls=%fused_computation.19 | loop fusion | flops 1566720 | bytes 4218880 | tf_op jit(solution)/shard_map/reduce_sum | solution.py:138
  36.6 2.3 collective-permute-done
  53.3 13.7 %all-gather = f32[32,3,256]{2,0,1:T(8,128)S(1)} all-gather(f32[8,3,256]{2,0,1:T(8,128)S(1)} %get-tuple-element.714), channel_id=2, replica_groups=mesh['surf'=8,'norm'=4] {'norm'}, dimensions={0}, use_global_device_ids=true | all-gather | bytes 122880 | tf_op jit(solution)/shard_map/all_gather | solution.py:41
  68.4 14.3 %all_gather.16 = f32[4,8,9,256]{3,1,2,0:T(8,128)S(1)} all-gather(f32[1,8,9,256]{3,1,2,0:T(8,128)S(1)} %bitcast.936), channel_id=1, replica_groups=mesh['surf'=8,'norm'=4] {'norm'}, dimensions={0}, use_global_device_ids=true | all-gather | bytes 368640 | tf_op jit(solution)/shard_map/all_gather | solution.py:41
  86.1 14.3 %all_gather.36 = f32[4,8,9,256]{3,1,2,0:T(8,128)S(1)} all-gather(f32[1,8,9,256]{3,1,2,0:T(8,128)S(1)} %bitcast.935), channel_id=1, replica_groups=mesh['surf'=8,'norm'=4] {'norm'}, dimensions={0}, use_global_device_ids=true | all-gather | bytes 368640 | tf_op jit(solution)/shard_map/all_gather | solution.py:41
  100.4 14.0 %all_gather.37 = f32[4,8,3,256]{3,1,2,0:T(8,128)} all-gather(f32[1,8,3,256]{3,1,2,0:T(8,128)S(1)} %get-tuple-element.635), channel_id=1, replica_groups=mesh['surf'=8,'norm'=4] {'norm'}, dimensions={0}, use_global_device_ids=true | all-gather | bytes 122880 | tf_op jit(solution)/shard_map/all_gather | solution.py:41
  115.0 6.3 %while.82 = (s32[]{:T(128)}, f32[8,3,256]{2,0,1:T(8,128)}, s32[]{:T(128)}, f32[4,8,9,256]{3,1,2,0:T(8,128)S(1)}, f32[4,8,3,256]{3,1,2,0:T(8,128)}, /*index=5*/s32[]{:T(128)}, s32[]{:T(128)}, s32[]{:T(128)}, s32[]{:T(128)}) while((s32[]{:T(128)}, f32[8,3,256]{2,0,1:T(8,128)}, s32[]{:T(128)}, f32[4,8,9,256]{3,1,2,0:T(8,128)S(1)}, ...), condition=%wide.region_71.72_spmd, body=%wide.region_69.71_spmd.sunk | while | flops 36870 | bytes 344219 | solution.py:50
  115.7 1.4 bitcast_add_fusion.103
  117.9 1.4 bitcast_add_fusion.103
  123.1 1.7 fusion.115
  125.3 1.8 collective-permute-done.4
  127.1 2.5 %collective-permute-done.3 = bf16[16,1,3,256]{3,1,2,0:T(2,128)(2,1)} collective-permute-done((bf16[16,1,3,256]{3,1,2,0:T(2,128)(2,1)}, bf16[16,1,3,256]{3,1,2,0:T(2,128)(2,1)}, u32[]{:S(2)}, u32[]{:S(2)}) %collective-permute-start.3) | collective-permute-done | bytes 24608 | tf_op jit(solution)/shard_map/ppermute | solution.py:29
  141.5 14.0 %all-gather.1 = f32[32,3,256]{2,0,1:T(8,128)} all-gather(f32[8,3,256]{2,0,1:T(8,128)S(1)} %multiply_reduce_fusion.90), channel_id=3, replica_groups=mesh['surf'=8,'norm'=4] {'norm'}, dimensions={0}, use_global_device_ids=true | all-gather | bytes 122880 | tf_op jit(solution)/shard_map/all_gather | solution.py:41
  160.9 16.5 %all_gather.39 = f32[4,8,3,256]{3,1,2,0:T(8,128)} all-gather(f32[1,8,3,256]{3,1,2,0:T(8,128)S(1)} %get-tuple-element.633), channel_id=1, replica_groups=mesh['surf'=8,'norm'=4] {'norm'}, dimensions={0}, use_global_device_ids=true | all-gather | bytes 122880 | tf_op jit(solution)/shard_map/all_gather | solution.py:41
  178.1 6.3 %while.84 = (s32[]{:T(128)}, f32[8,3,256]{2,0,1:T(8,128)}, s32[]{:T(128)}, f32[4,8,9,256]{3,1,2,0:T(8,128)S(1)}, f32[4,8,3,256]{3,1,2,0:T(8,128)}, /*index=5*/s32[]{:T(128)}, s32[]{:T(128)}, s32[]{:T(128)}, s32[]{:T(128)}) while((s32[]{:T(128)}, f32[8,3,256]{2,0,1:T(8,128)}, s32[]{:T(128)}, f32[4,8,9,256]{3,1,2,0:T(8,128)S(1)}, ...), condition=%wide.region_110.111_spmd, body=%wide.region_108.110_spmd.sunk | while | flops 36870 | bytes 344219 | solution.py:50
  186.1 1.7 fusion.114
  188.4 1.8 collective-permute-done.6
  190.1 2.5 %collective-permute-done.5 = bf16[16,1,3,256]{3,1,2,0:T(2,128)(2,1)} collective-permute-done((bf16[16,1,3,256]{3,1,2,0:T(2,128)(2,1)}, bf16[16,1,3,256]{3,1,2,0:T(2,128)(2,1)}, u32[]{:S(2)}, u32[]{:S(2)}) %collective-permute-start.5) | collective-permute-done | bytes 24608 | tf_op jit(solution)/shard_map/ppermute | solution.py:29
  204.6 14.0 %all-gather.2 = f32[32,3,256]{2,0,1:T(8,128)} all-gather(f32[8,3,256]{2,0,1:T(8,128)S(1)} %multiply_reduce_fusion.59), channel_id=4, replica_groups=mesh['surf'=8,'norm'=4] {'norm'}, dimensions={0}, use_global_device_ids=true | all-gather | bytes 122880 | tf_op jit(solution)/shard_map/all_gather | solution.py:41
  223.3 15.8 %all_gather.41 = f32[4,8,3,256]{3,1,2,0:T(8,128)S(1)} all-gather(f32[1,8,3,256]{3,1,2,0:T(8,128)S(1)} %get-tuple-element.631), channel_id=1, replica_groups=mesh['surf'=8,'norm'=4] {'norm'}, dimensions={0}, use_global_device_ids=true | all-gather | bytes 122880 | tf_op jit(solution)/shard_map/all_gather | solution.py:41
  (727 shorter events, 74.2 us)
Async XLA Ops:
  0.0 12.9 %copy-start = (s32[64,256]{1,0:T(8,128)S(1)}, s32[64,256]{1,0:T(8,128)}, u32[]{:S(2)}) copy-start(s32[64,256]{1,0:T(8,128)} %param.30) | copy-start | bytes 196612
  3.5 7.5 %copy-start.148 = (f32[128]{0:T(128)S(1)}, f32[128]{0:T(128)}, u32[]{:S(2)}) copy-start(f32[128]{0:T(128)} %param.28) | copy-start | bytes 1540
  3.5 7.6 %copy-start.149 = (s32[128]{0:T(128)S(1)}, s32[128]{0:T(128)}, u32[]{:S(2)}) copy-start(s32[128]{0:T(128)} %param.29) | copy-start | bytes 1540
  3.5 7.7 %copy-start.146 = (s32[8,256]{1,0:T(8,128)S(1)}, s32[8,256]{1,0:T(8,128)}, u32[]{:S(2)}) copy-start(s32[8,256]{1,0:T(8,128)} %param.31) | copy-start | bytes 24580
  3.5 26.3 %all-to-all-start = ((bf16[16,64,3,256]{3,0,2,1:T(8,128)(2,1)}), bf16[16,64,3,256]{3,0,2,1:T(8,128)(2,1)S(1)}, u32[]{:S(2)}, u32[]{:S(2)}) async-start(bf16[16,64,3,256]{3,0,2,1:T(8,128)(2,1)} %copy.1008), calls=%async_computation | async-start | bytes 3145728 | tf_op jit(solution)/shard_map/all_to_all | solution.py:131
  9.6 32.4 %copy-start.48 = (f32[8,256]{1,0:T(8,128)}, f32[8,256]{1,0:T(8,128)S(1)}, u32[]{:S(2)}) copy-start(f32[8,256]{1,0:T(8,128)S(1)} %get-tuple-element.680) | copy-start | bytes 24580
  9.6 32.5 %copy-start.54 = (f32[8,256]{1,0:T(8,128)}, f32[8,256]{1,0:T(8,128)S(1)}, u32[]{:S(2)}) copy-start(f32[8,256]{1,0:T(8,128)S(1)} %get-tuple-element.679) | copy-start | bytes 24580
  9.6 33.3 %copy-start.60 = (f32[8,256]{1,0:T(8,128)}, f32[8,256]{1,0:T(8,128)S(1)}, u32[]{:S(2)}) copy-start(f32[8,256]{1,0:T(8,128)S(1)} %get-tuple-element.678) | copy-start | bytes 24580
  9.6 34.1 %copy-start.66 = (f32[8,256]{1,0:T(8,128)}, f32[8,256]{1,0:T(8,128)S(1)}, u32[]{:S(2)}) copy-start(f32[8,256]{1,0:T(8,128)S(1)} %get-tuple-element.677) | copy-start | bytes 24580
  9.6 34.9 %copy-start.72 = (f32[8,256]{1,0:T(8,128)}, f32[8,256]{1,0:T(8,128)S(1)}, u32[]{:S(2)}) copy-start(f32[8,256]{1,0:T(8,128)S(1)} %get-tuple-element.676) | copy-start | bytes 24580
  9.6 35.7 %copy-start.78 = (f32[8,256]{1,0:T(8,128)}, f32[8,256]{1,0:T(8,128)S(1)}, u32[]{:S(2)}) copy-start(f32[8,256]{1,0:T(8,128)S(1)} %get-tuple-element.675) | copy-start | bytes 24580
  9.7 36.5 %copy-start.84 = (f32[8,256]{1,0:T(8,128)}, f32[8,256]{1,0:T(8,128)S(1)}, u32[]{:S(2)}) copy-start(f32[8,256]{1,0:T(8,128)S(1)} %get-tuple-element.674) | copy-start | bytes 24580
  9.7 25.3 %collective-permute-start.2 = (f32[8,256]{1,0:T(8,128)}, f32[8,256]{1,0:T(8,128)}, u32[]{:S(2)}, u32[]{:S(2)}) collective-permute-start(f32[8,256]{1,0:T(8,128)} %get-tuple-element.681), channel_id=1, source_target_pairs={{1,0},{2,1},{3,2},{5,4},{6,5},{7,6},{9,8},{10,9},{11,10},{13,12},{... | collective-permute-start | bytes 24584 | tf_op jit(solution)/shard_map/ppermute | solution.py:12
  15.9 68.1 %copy-start.16 = (f32[1,8,9,256]{3,1,2,0:T(8,128)}, f32[1,8,9,256]{3,1,2,0:T(8,128)S(1)}, u32[]{:S(2)}) copy-start(f32[1,8,9,256]{3,1,2,0:T(8,128)S(1)} %get-tuple-element.642) | copy-start | bytes 221188
  15.9 68.2 %copy-start.11 = (f32[1,8,9,256]{3,1,2,0:T(8,128)}, f32[1,8,9,256]{3,1,2,0:T(8,128)S(1)}, u32[]{:S(2)}) copy-start(f32[1,8,9,256]{3,1,2,0:T(8,128)S(1)} %get-tuple-element.643) | copy-start | bytes 221188
  15.9 68.2 %copy-start.6 = (f32[1,8,9,256]{3,1,2,0:T(8,128)}, f32[1,8,9,256]{3,1,2,0:T(8,128)S(1)}, u32[]{:S(2)}) copy-start(f32[1,8,9,256]{3,1,2,0:T(8,128)S(1)} %get-tuple-element.644) | copy-start | bytes 221188
  15.9 68.3 %copy-start.1 = (f32[1,8,9,256]{3,1,2,0:T(8,128)}, f32[1,8,9,256]{3,1,2,0:T(8,128)S(1)}, u32[]{:S(2)}) copy-start(f32[1,8,9,256]{3,1,2,0:T(8,128)S(1)} %get-tuple-element.645) | copy-start | bytes 221188
  34.4 2.2 collective-permute-start.1
  34.5 4.5 %collective-permute-start = (bf16[16,1,3,256]{3,1,2,0:T(2,128)(2,1)S(1)}, bf16[16,1,3,256]{3,1,2,0:T(2,128)(2,1)S(1)}, u32[]{:S(2)}, u32[]{:S(2)}) collective-permute-start(bf16[16,1,3,256]{3,1,2,0:T(2,128)(2,1)S(1)} %get-tuple-element.664), channel_id=1, source_target_pairs={{0,4},{4,8},{8,12},{12,16},{16,20},{20,24},{24,28},{28,0},{1,5},{5... | collective-permute-start | bytes 73736 | tf_op jit(solution)/shard_map/ppermute | solution.py:29
  47.8 19.2 %copy-start.144 = (f32[3,3]{1,0:T(4,128)S(1)}, f32[3,3]{1,0:T(4,128)}, u32[]{:S(2)}) copy-start(f32[3,3]{1,0:T(4,128)} %fusion.108) | copy-start | bytes 112
  124.8 2.3 collective-permute-start.4
  124.8 4.7 %collective-permute-start.3 = (bf16[16,1,3,256]{3,1,2,0:T(2,128)(2,1)}, bf16[16,1,3,256]{3,1,2,0:T(2,128)(2,1)}, u32[]{:S(2)}, u32[]{:S(2)}) collective-permute-start(bf16[16,1,3,256]{3,1,2,0:T(2,128)(2,1)} %get-tuple-element.662), channel_id=1, source_target_pairs={{0,4},{4,8},{8,12},{12,16},{16,20},{20,24},{24,28},{28,0},{1,5},{5... | collective-permute-start | bytes 73736 | tf_op jit(solution)/shard_map/ppermute | solution.py:29
  187.9 2.3 collective-permute-start.6
  187.9 4.7 %collective-permute-start.5 = (bf16[16,1,3,256]{3,1,2,0:T(2,128)(2,1)}, bf16[16,1,3,256]{3,1,2,0:T(2,128)(2,1)}, u32[]{:S(2)}, u32[]{:S(2)}) collective-permute-start(bf16[16,1,3,256]{3,1,2,0:T(2,128)(2,1)} %get-tuple-element.660), channel_id=1, source_target_pairs={{0,4},{4,8},{8,12},{12,16},{16,20},{20,24},{24,28},{28,0},{1,5},{5... | collective-permute-start | bytes 73736 | tf_op jit(solution)/shard_map/ppermute | solution.py:29
  (134 other events, 427.0 us)
where the time goes:
time: 243 us; the launch traced here: 240 us
  blocking collectives  117 us (48%)
  other arithmetic  47.9 us (20%)
  local copies, waits for them, and re-layouts  37.9 us (16%)
  waiting for transfers between devices  25.7 us (11%)
  starting transfers between devices  8.21 us (3%)
  between operations  3.76 us (2%)
    all_gather x8, blocking collectives, carried_in(): gathered = jax.tree.map(lambda a: lax.all_gather(a, axis), part)  117 us
    unnamed x376, local copies, waits for them, and re-layouts  27.2 us
    all_to_all x1, waiting for transfers between devices, per_device(): lax.all_to_all(mode_shapes, 'surf', split_axis=1, concat_axis=0, tiled=True)  14 us
    add x48, other arithmetic, forward(): right_side[cell] + lower_link[cell][:, None, :] * state_now  11.4 us
    reduce_sum x77, other arithmetic, mat_vec(): return jnp.sum(blocks * vector[..., None, :, :], axis=-2)  9.06 us
    add x9, other arithmetic, compose(): mat_vec(later_map, earlier_shift) + later_shift  8.16 us
    ppermute x3, waiting for transfers between devices, padded_2(): lax.ppermute(lax.slice_in_dim(block, block.shape[dim] - width, None, axis...  7.25 us
    all_to_all x1, starting transfers between devices, per_device(): lax.all_to_all(mode_shapes, 'surf', split_axis=1, concat_axis=0, tiled=True)  5.34 us
  transfers between devices with their start and end apart: 8, of which 7 were waited for; matrix products, arithmetic and copies ran while one was open for 4% of the time, Pallas kernels for 0%

commit v1 on v0

v1 whole, which is shorter than its diff:
```python
import functools

import jax
import jax.numpy as jnp
from jax import lax
from jax.experimental import pallas as pl
from jax.experimental.pallas import tpu as pltpu
from jax.sharding import PartitionSpec as P

SWEEPS = 3
MESH = pl.DeviceIdType.MESH


def loop(count, body, init, unroll=4):
    if count % unroll:
        unroll = 1

    def outer(step, carry):
        for part in range(unroll):
            carry = body(step * unroll + part, carry)
        return carry

    return lax.fori_loop(0, count // unroll, outer, init)


def mat_vec(matrix, vector):
    return [
        matrix[3 * a] * vector[0] + matrix[3 * a + 1] * vector[1] + matrix[3 * a + 2] * vector[2]
        for a in range(3)
    ]


def mat_mat(left, right):
    return [
        left[3 * a] * right[b] + left[3 * a + 1] * right[3 + b] + left[3 * a + 2] * right[6 + b]
        for a in range(3)
        for b in range(3)
    ]


def added(left, right):
    return [a + b for a, b in zip(left, right)]


def planes(ref, index, count=3):
    return [ref[index, c] for c in range(count)]


def put(ref, index, values):
    for c, value in enumerate(values):
        ref[index, c] = value


def kernel(
    surf_size,
    norm_size,
    amplitude,
    mode_patch,
    column_patch,
    wall_mask,
    offsets,
    modes_hbm,
    coupling_hbm,
    pivot_hbm,
    stiffness_hbm,
    out,
    modes,
    coupling,
    pivot,
    stiffness,
    link,
    link_next,
    maps,
    end_map,
    part,
    got,
    mask_edge,
    wall,
    values,
    edge,
    edge_out,
    edge_in,
    halo,
    f_in,
    f_out,
    o_in,
    o_out,
    o_true,
    h_in,
    h_out,
    load_sem,
    part_send,
    part_recv,
    mask_send,
    mask_recv,
    link_send,
    link_recv,
    h_send,
    h_recv,
    f_send,
    f_recv,
    o_send,
    o_recv,
    edge_send,
    edge_recv,
):
    S, N = surf_size, norm_size
    half = N // 2
    K, _, R, W = pivot.shape
    M = modes.shape[0]
    B = 2 * R
    blocks = modes.shape[2] // B
    me = lax.axis_index("surf")
    place = lax.axis_index("norm")
    before = lax.rem(me + S - 1, S)
    after = lax.rem(me + 1, S)
    first, last = place == 0, place == N - 1

    def to_surf(src, dst, send, recv, target):
        return pltpu.make_async_remote_copy(
            src_ref=src, dst_ref=dst, send_sem=send, recv_sem=recv,
            device_id={"surf": target}, device_id_type=MESH,
        )

    def to_norm(src, dst, send, recv, target):
        return pltpu.make_async_remote_copy(
            src_ref=src, dst_ref=dst, send_sem=send, recv_sem=recv,
            device_id={"norm": target}, device_id_type=MESH,
        )

    mode_loads = [
        pltpu.make_async_copy(
            modes_hbm.at[:, :, pl.ds(b * B, B), :], modes.at[:, :, pl.ds(b * B, B), :], load_sem.at[3 + b]
        )
        for b in range(blocks)
    ]
    loads = [
        pltpu.make_async_copy(coupling_hbm, coupling, load_sem.at[0]),
        pltpu.make_async_copy(pivot_hbm, pivot, load_sem.at[1]),
        pltpu.make_async_copy(stiffness_hbm, stiffness, load_sem.at[2]),
    ]
    for copy in mode_loads + loads:
        copy.start()

    barrier = pltpu.get_barrier_semaphore()
    for hop in range(1, S):
        pl.semaphore_signal(
            barrier, inc=1, device_id={"surf": lax.rem(me + hop, S)}, device_id_type=MESH
        )

    @pl.when(jnp.logical_not(first))
    def _():
        pl.semaphore_signal(barrier, inc=1, device_id={"norm": place - 1}, device_id_type=MESH)

    @pl.when(jnp.logical_not(last))
    def _():
        pl.semaphore_signal(barrier, inc=1, device_id={"norm": place + 1}, device_id_type=MESH)

    own_mode = me * M
    for b in range(blocks):
        mode_loads[b].wait()
        patch = column_patch[b * B : (b + 1) * B, :]

        def mode_step(m, sums):
            weight = jnp.where(
                patch == mode_patch[own_mode + m], amplitude[own_mode + m], jnp.float32(0)
            )
            return [
                sums[c] + weight * modes[m, c, b * B : (b + 1) * B, :].astype(jnp.float32)
                for c in range(3)
            ]

        sums = loop(M, mode_step, [jnp.zeros((B, W), jnp.float32)] * 3)
        for c in range(3):
            for side in range(2):
                dest = 2 * b + side
                block = sums[c][side * R : (side + 1) * R]
                part[dest, c] = block
                part[(dest + 1) % S, 3, c : c + 1, :] = block[R - 1 : R]
                part[(dest - 1) % S, 3, 3 + c : 4 + c, :] = block[0:1]

    @pl.when(jnp.logical_or(first, last))
    def _():
        pl.semaphore_wait(barrier, S)

    @pl.when(jnp.logical_not(jnp.logical_or(first, last)))
    def _():
        pl.semaphore_wait(barrier, S + 1)

    def part_copy(hop):
        dest = lax.rem(me + hop, S)
        return to_surf(part.at[dest], got.at[hop], part_send.at[hop], part_recv.at[hop], dest)

    for hop in range(1, S):
        part_copy(hop).start()
    mask_up = to_surf(wall_mask, mask_edge.at[0], mask_send.at[0], mask_recv.at[0], after)
    mask_down = to_surf(wall_mask, mask_edge.at[1], mask_send.at[1], mask_recv.at[1], before)
    mask_up.start()
    mask_down.start()
    link_copy = to_norm(coupling_hbm.at[0], link_next, link_send, link_recv, place - 1)

    @pl.when(jnp.logical_not(first))
    def _():
        link_copy.start()

    for copy in loads:
        copy.wait()
    cut = offsets[...]
    base = place * K

    def link_step(k, carry):
        link[k] = jnp.where(cut == base + k, jnp.float32(0), coupling[k])
        return carry

    loop(K, link_step, 0)

    @pl.when(last)
    def _():
        link[K] = jnp.zeros((R, W), jnp.float32)

    def lower_step(k, state):
        scaled = [p * link[k] for p in planes(pivot, k, 9)]
        state = mat_mat(scaled, state)
        put(maps, k, state)
        return state

    first_map = [p * link[0] for p in planes(pivot, 0, 9)]
    put(maps, 0, first_map)
    ends = lax.fori_loop(1, K, lower_step, first_map)
    for c in range(9):
        end_map[c] = ends[c]

    @pl.when(jnp.logical_not(last))
    def _():
        link_copy.wait_recv()
        link[K] = jnp.where(cut == base + K, jnp.float32(0), link_next[...])

    def upper_step(step, state):
        k = K - 1 - step
        scaled = [p * link[k + 1] for p in planes(pivot, k, 9)]
        state = added(planes(maps, k, 9), mat_mat(scaled, state[:9])) + mat_mat(scaled, state[9:])
        put(maps, k, state)
        return state

    top_link = link[K]
    top_state = planes(maps, K - 1, 9) + [p * top_link for p in planes(pivot, K - 1, 9)]
    put(maps, K - 1, top_state)
    top_state = lax.fori_loop(1, K, upper_step, top_state)

    h_copy = to_norm(h_out, h_in, h_send, h_recv, place - 1)
    gets_h = jnp.logical_and(place >= half - 1, jnp.logical_not(last))

    @pl.when(gets_h)
    def _():
        h_copy.wait_recv()

    @pl.when(jnp.logical_not(gets_h))
    def _():
        h_in[...] = jnp.zeros((9, R, W), jnp.float32)

    @pl.when(place >= half)
    def _():
        inner = mat_mat([h_in[c] for c in range(9)], [end_map[c] for c in range(9)])
        whole = added(planes(maps, 0, 9), mat_mat([maps[0, 9 + c] for c in range(9)], inner))
        for c in range(9):
            h_out[c] = whole[c]
        h_copy.start()

    @pl.when(first)
    def _():
        f_in[...] = jnp.zeros(f_in.shape, jnp.float32)

    @pl.when(last)
    def _():
        o_in[...] = jnp.zeros(o_in.shape, jnp.float32)

    total = [part[me, c] for c in range(4)]
    mask_up.wait_recv()
    mask_down.wait_recv()
    for hop in range(1, S):
        part_copy(hop).wait_recv()
        total = [total[c] + got[hop, c] for c in range(4)]
    mask = wall_mask[...].astype(jnp.float32)
    low_mask = mask_edge[0, R - 1 : R, :].astype(jnp.float32)
    high_mask = mask_edge[1, 0:1, :].astype(jnp.float32)
    row = lax.broadcasted_iota(jnp.int32, (R, W), 0)
    lane = lax.broadcasted_iota(jnp.int32, (R, W), 1)

    def around(x, low, high):
        nearby = jnp.where(row == 0, low, pltpu.roll(x, 1, 0))
        nearby += jnp.where(row == R - 1, high, pltpu.roll(x, R - 1, 0))
        nearby += jnp.where(lane == 0, jnp.float32(0), pltpu.roll(x, 1, 1))
        return nearby + jnp.where(lane == W - 1, jnp.float32(0), pltpu.roll(x, W - 1, 1))

    at_wall = jnp.where(first, jnp.float32(1), jnp.float32(0))
    for c in range(3):
        shift = total[c] * mask
        wall[c] = link[0] * shift * at_wall
        wall[3 + c] = around(
            shift, total[3][c : c + 1] * low_mask, total[3][3 + c : 4 + c] * high_mask
        )

    def edge_copies(sweep):
        return [
            to_surf(edge_out.at[sweep, 1], edge_in.at[sweep, 0], edge_send.at[sweep, 0], edge_recv.at[sweep, 0], after),
            to_surf(edge_out.at[sweep, 0], edge_in.at[sweep, 1], edge_send.at[sweep, 1], edge_recv.at[sweep, 1], before),
        ]

    def chain_copies(sweep):
        return (
            to_norm(f_out.at[sweep], f_in.at[sweep], f_send.at[sweep], f_recv.at[sweep], place + 1),
            to_norm(o_out.at[sweep], o_in.at[sweep], o_send.at[sweep], o_recv.at[sweep], place - 1),
        )

    for sweep in range(SWEEPS):
        if sweep > 0:
            for copy in edge_copies(sweep - 1):
                copy.wait_recv()
            for side in range(2):
                halo[side] = edge_in[sweep - 1, side].astype(jnp.float32)

        def source(k, sweep=sweep):
            if sweep == 0:
                blend = 1.0 - (base + k).astype(jnp.float32) / (K * N)
                factor = stiffness[k] * blend
                return [factor * wall[3 + c] for c in range(3)]
            return [
                stiffness[k]
                * around(out[k, c], halo[0, c, pl.ds(k, 1), :], halo[1, c, pl.ds(k, 1), :])
                for c in range(3)
            ]

        def forward(k, state):
            right = added(source(k), [link[k] * s for s in state])
            state = mat_vec(planes(pivot, k, 9), right)
            put(values, k, state)
            return state

        start = mat_vec(
            planes(pivot, 0, 9), added(source(0), [wall[c] for c in range(3)])
        )
        put(values, 0, start)
        ends = lax.fori_loop(1, K, forward, start)

        def backward(step, state):
            k = K - 1 - step
            state = added(
                planes(values, k), mat_vec(planes(pivot, k, 9), [link[k + 1] * s for s in state])
            )
            put(values, k, state)
            return state

        tops = lax.fori_loop(1, K, backward, ends)
        for c in range(3):
            edge[0, c] = ends[c]
            edge[1, c] = tops[c]

        f_copy, o_copy = chain_copies(sweep)

        def own(which):
            return [edge[which, c] for c in range(3)]

        def end_state(entering):
            return added(own(0), mat_vec([end_map[c] for c in range(9)], entering))

        def leaving(state):
            return added(
                planes(o_in, sweep), mat_vec([h_in[c] for c in range(9)], state)
            )

        @pl.when(place < half)
        def _():
            @pl.when(jnp.logical_not(first))
            def _():
                f_copy.wait_recv()

            entering = planes(f_in, sweep)
            state = end_state(entering)
            put(f_out, sweep, state)
            f_copy.start()
            o_copy.wait_recv()
            above = leaving(state)
            for c in range(3):
                o_true[c] = above[c]

            @pl.when(jnp.logical_not(first))
            def _():
                top = added(own(1), mat_vec([maps[0, c] for c in range(9)], entering))
                top = added(top, mat_vec([maps[0, 9 + c] for c in range(9)], above))
                put(o_out, sweep, top)
                o_copy.start()

        @pl.when(place >= half)
        def _():
            @pl.when(jnp.logical_not(last))
            def _():
                o_copy.wait_recv()

            top = added(
                own(1), mat_vec([maps[0, 9 + c] for c in range(9)], leaving(own(0)))
            )
            put(o_out, sweep, top)
            o_copy.start()
            f_copy.wait_recv()
            state = end_state(planes(f_in, sweep))

            @pl.when(jnp.logical_not(last))
            def _():
                put(f_out, sweep, state)
                f_copy.start()

            above = leaving(state)
            for c in range(3):
                o_true[c] = above[c]

        entering = planes(f_in, sweep)
        above = [o_true[c] for c in range(3)]

        def finish(k, carry, sweep=sweep):
            state = added(planes(values, k), mat_vec(planes(maps, k, 9), entering))
            state = added(state, mat_vec([maps[k, 9 + c] for c in range(9)], above))
            put(out, k, state)
            if sweep < SWEEPS - 1:
                for c in range(3):
                    halo[0, c, pl.ds(k, 1), :] = state[c][0:1]
                    halo[1, c, pl.ds(k, 1), :] = state[c][R - 1 : R]
            return carry

        loop(K, finish, 0, 2)
        if sweep < SWEEPS - 1:
            for side in range(2):
                edge_out[sweep, side] = halo[side].astype(jnp.bfloat16)
            for copy in edge_copies(sweep):
                copy.start()

    for hop in range(1, S):
        part_copy(hop).wait_send()
    mask_up.wait_send()
    mask_down.wait_send()
    for sweep in range(SWEEPS - 1):
        for copy in edge_copies(sweep):
            copy.wait_send()

    @pl.when(place >= half)
    def _():
        h_copy.wait_send()

    @pl.when(jnp.logical_not(first))
    def _():
        link_copy.wait_send()
        for sweep in range(SWEEPS):
            chain_copies(sweep)[1].wait_send()

    @pl.when(jnp.logical_not(last))
    def _():
        for sweep in range(SWEEPS):
            chain_copies(sweep)[0].wait_send()


def per_device(
    surf_size, norm_size, mode_shapes, amplitude, mode_patch, column_patch, wall_mask, offsets,
    coupling, pivot_inv, stiffness,
):
    S = surf_size
    modes = mode_shapes.transpose(0, 2, 1, 3)
    pivot = pivot_inv.transpose(0, 2, 1, 3)
    K, _, R, W = pivot.shape
    f32, bf16 = jnp.float32, jnp.bfloat16
    vmem = pl.BlockSpec(memory_space=pltpu.VMEM)
    smem = pl.BlockSpec(memory_space=pltpu.SMEM)
    hbm = pl.BlockSpec(memory_space=pl.ANY)
    dma = pltpu.SemaphoreType.DMA
    out = pl.pallas_call(
        functools.partial(kernel, surf_size, norm_size),
        out_shape=jax.ShapeDtypeStruct((K, 3, R, W), f32),
        in_specs=[smem, smem, vmem, vmem, vmem, hbm, hbm, hbm, hbm],
        out_specs=vmem,
        scratch_shapes=[
            pltpu.VMEM(modes.shape, bf16),
            pltpu.VMEM((K, R, W), f32),
            pltpu.VMEM((K, 9, R, W), f32),
            pltpu.VMEM((K, R, W), f32),
            pltpu.VMEM((K + 1, R, W), f32),
            pltpu.VMEM((R, W), f32),
            pltpu.VMEM((K, 18, R, W), f32),
            pltpu.VMEM((9, R, W), f32),
            pltpu.VMEM((S, 4, R, W), f32),
            pltpu.VMEM((S, 4, R, W), f32),
            pltpu.VMEM((2, R, W), jnp.int32),
            pltpu.VMEM((6, R, W), f32),
            pltpu.VMEM((K, 3, R, W), f32),
            pltpu.VMEM((2, 3, R, W), f32),
            pltpu.VMEM((SWEEPS - 1, 2, 3, K, W), bf16),
            pltpu.VMEM((SWEEPS - 1, 2, 3, K, W), bf16),
            pltpu.VMEM((2, 3, K, W), f32),
            pltpu.VMEM((SWEEPS, 3, R, W), f32),
            pltpu.VMEM((SWEEPS, 3, R, W), f32),
            pltpu.VMEM((SWEEPS, 3, R, W), f32),
            pltpu.VMEM((SWEEPS, 3, R, W), f32),
            pltpu.VMEM((3, R, W), f32),
            pltpu.VMEM((9, R, W), f32),
            pltpu.VMEM((9, R, W), f32),
            dma((3 + modes.shape[2] // (2 * R),)),
            dma((S,)),
            dma((S,)),
            dma((2,)),
            dma((2,)),
            dma,
            dma,
            dma,
            dma,
            dma((SWEEPS,)),
            dma((SWEEPS,)),
            dma((SWEEPS,)),
            dma((SWEEPS,)),
            dma((SWEEPS - 1, 2)),
            dma((SWEEPS - 1, 2)),
        ],
        compiler_params=pltpu.CompilerParams(collective_id=0, has_side_effects=True),
        name="line_sweeps",
    )(amplitude, mode_patch, column_patch, wall_mask, offsets, modes, coupling, pivot, stiffness)
    return out.transpose(0, 2, 1, 3)


def solution(mesh):
    return jax.shard_map(
        functools.partial(per_device, mesh.shape["surf"], mesh.shape["norm"]),
        mesh=mesh,
        in_specs=(
            P("surf", None, None, None),
            P(),
            P(),
            P(),
            P("surf", None),
            P("surf", None),
            P("norm", "surf", None),
            P("norm", "surf", None, None),
            P("norm", "surf", None),
        ),
        out_specs=P("norm", "surf", None, None),
        check_vma=False,
    )
```

time: 243 us -> 47.5 us (0.20); the launches traced: 240 us -> 47.3 us
  blocking collectives: 117 us -> 0 us
  other arithmetic: 47.9 us -> 0 us
  Pallas kernels: 0 us -> 45.5 us
  local copies, waits for them, and re-layouts: 37.9 us -> 1.77 us
  waiting for transfers between devices: 25.7 us -> 0 us
  starting transfers between devices: 8.21 us -> 0 us
  between operations: 3.76 us -> 0.01 us
    all_gather x8 -> x0, blocking collectives: 117 us -> none  [carried_in(): gathered = jax.tree.map(lambda a: lax.all_gather(a, axis), part)]
    pallas_call x0 -> x1, Pallas kernels: none -> 45.5 us  [per_device(): pl.pallas_call(functools.partial(kernel, surf_size, norm_size), out_shape...]
    unnamed x376 -> x1, local copies, waits for them, and re-layouts: 27.2 us -> 1.77 us
    add x62 -> x0, other arithmetic: 22.9 us -> none  [the longest x48 11.4 us: forward(): right_side[cell] + lower_link[cell][:, None, :] * state_now]
    reduce_sum x109 -> x0, other arithmetic: 14.3 us -> none  [the longest x77 9.06 us: mat_vec(): return jnp.sum(blocks * vector[..., None, :, :], axis=-2)]
    all_to_all x1 -> x0, waiting for transfers between devices: 14 us -> none  [per_device(): lax.all_to_all(mode_shapes, 'surf', split_axis=1, concat_axis=0, tiled=True)]
    ppermute x7 -> x0, waiting for transfers between devices: 11.7 us -> none  [the longest x3 7.25 us: padded_2(): lax.ppermute(lax.slice_in_dim(block, block.shape[dim] - width, None, axis...]
    slice x7 -> x0, local copies, waits for them, and re-layouts: 6.18 us -> none  [the longest x3 3.54 us: padded_2(): lax.slice_in_dim(block, block.shape[dim] - width, None, axis=dim)]
  transfers between devices with their start and end apart: 8 -> 0, of which waited for: 7 -> 0; matrix products, arithmetic and copies ran while one was open for 4% -> 0% of each run, Pallas kernels for 0% -> 0%
where the time goes in v1:
time: 47.5 us; the launch traced here: 47.3 us
  Pallas kernels  45.5 us (96%)
  local copies, waits for them, and re-layouts  1.77 us (4%)
    pallas_call x1, Pallas kernels, per_device(): pl.pallas_call(functools.partial(kernel, surf_size, norm_size), out_shape...  45.5 us
    unnamed x1, local copies, waits for them, and re-layouts  1.77 us

profile of v1, /device:TPU:0, one launch (start us, length us, event | category | flops | bytes accessed | tf_op | source)
XLA Modules:
  0.0 47.3 jit_solution(10223103220579361900)
XLA Ops:
  0.0 45.5 %line_sweeps.1 = f32[16,3,8,256]{3,2,1,0:T(8,128)} custom-call(f32[128]{0:T(128)} %amplitude.1, s32[128]{0:T(128)} %mode_patch.1, s32[64,256]{1,0:T(8,128)} %column_patch.1, s32[8,256]{1,0:T(8,128)} %wall_mask.1, s32[8,256]{1,0:T(8,128)} %offsets.1, bf16[16,3,64,256]{3,2,1,0:T(8,128)(2,1)} %bitcast.3, f32[16,8,256]{2,1,0:T(8,128)} %coupling_hbm.1, ...), custom_call_target="tpu_custom_call" | custom-call | tf_op jit(solution)/shard_map/line_sweeps/pallas_call | solution.py:473
  45.5 1.8 %copy.11 = f32[16,8,3,256]{3,1,2,0:T(8,128)} copy(f32[16,8,3,256]{3,1,2,0:T(8,128)} %bitcast.4) | data formatting | bytes 786432

commit v2 on v1

--- a/solution.py
+++ b/solution.py
@@ -77,7 +77,7 @@
     mask_edge,
     wall,
     values,
-    edge,
+    enter,
     edge_out,
     edge_in,
     halo,
@@ -85,9 +85,12 @@
     f_out,
     o_in,
     o_out,
-    o_true,
     h_in,
     h_out,
+    up_in,
+    up_out,
+    down_in,
+    down_out,
     load_sem,
     part_send,
     part_recv,
@@ -97,6 +100,10 @@
     link_recv,
     h_send,
     h_recv,
+    up_send,
+    up_recv,
+    down_send,
+    down_recv,
     f_send,
     f_recv,
     o_send,
@@ -105,7 +112,6 @@
     edge_recv,
 ):
     S, N = surf_size, norm_size
-    half = N // 2
     K, _, R, W = pivot.shape
     M = modes.shape[0]
     B = 2 * R
@@ -148,13 +154,10 @@
             barrier, inc=1, device_id={"surf": lax.rem(me + hop, S)}, device_id_type=MESH
         )
 
-    @pl.when(jnp.logical_not(first))
-    def _():
-        pl.semaphore_signal(barrier, inc=1, device_id={"norm": place - 1}, device_id_type=MESH)
-
-    @pl.when(jnp.logical_not(last))
-    def _():
-        pl.semaphore_signal(barrier, inc=1, device_id={"norm": place + 1}, device_id_type=MESH)
+    for hop in range(1, N):
+        pl.semaphore_signal(
+            barrier, inc=1, device_id={"norm": lax.rem(place + hop, N)}, device_id_type=MESH
+        )
 
     own_mode = me * M
     for b in range(blocks):
@@ -179,13 +182,7 @@
                 part[(dest + 1) % S, 3, c : c + 1, :] = block[R - 1 : R]
                 part[(dest - 1) % S, 3, 3 + c : 4 + c, :] = block[0:1]
 
-    @pl.when(jnp.logical_or(first, last))
-    def _():
-        pl.semaphore_wait(barrier, S)
-
-    @pl.when(jnp.logical_not(jnp.logical_or(first, last)))
-    def _():
-        pl.semaphore_wait(barrier, S + 1)
+    pl.semaphore_wait(barrier, S + N - 2)
 
     def part_copy(hop):
         dest = lax.rem(me + hop, S)
@@ -248,31 +245,72 @@
     top_state = lax.fori_loop(1, K, upper_step, top_state)
 
     h_copy = to_norm(h_out, h_in, h_send, h_recv, place - 1)
-    gets_h = jnp.logical_and(place >= half - 1, jnp.logical_not(last))
-
-    @pl.when(gets_h)
+    inside = jnp.logical_not(jnp.logical_or(first, last))
+
+    def up_map(j):
+        return to_norm(up_out.at[j], up_in.at[j], up_send.at[j], up_recv.at[j], place + 1)
+
+    def down_map(j):
+        return to_norm(down_out.at[j], down_in.at[j], down_send.at[j], down_recv.at[j], place - 1)
+
+    def sends_up(j):
+        return jnp.logical_and(place >= j, jnp.logical_not(last))
+
+    def sends_down(j):
+        return jnp.logical_and(N - 1 - place >= j, jnp.logical_not(first))
+
+    @pl.when(last)
+    def _():
+        h_in[...] = jnp.zeros((9, R, W), jnp.float32)
+        for c in range(9):
+            h_out[c] = maps[0, c]
+        h_copy.start()
+
+    for j in range(1, min(2, N - 1)):
+
+        @pl.when(sends_up(j))
+        def _():
+            put(up_out, j, [end_map[c] for c in range(9)])
+            up_map(j).start()
+
+        @pl.when(sends_down(j))
+        def _():
+            put(down_out, j, [maps[0, 9 + c] for c in range(9)])
+            down_map(j).start()
+
+    @pl.when(inside)
     def _():
         h_copy.wait_recv()
-
-    @pl.when(jnp.logical_not(gets_h))
-    def _():
-        h_in[...] = jnp.zeros((9, R, W), jnp.float32)
-
-    @pl.when(place >= half)
-    def _():
         inner = mat_mat([h_in[c] for c in range(9)], [end_map[c] for c in range(9)])
         whole = added(planes(maps, 0, 9), mat_mat([maps[0, 9 + c] for c in range(9)], inner))
         for c in range(9):
             h_out[c] = whole[c]
         h_copy.start()
 
-    @pl.when(first)
-    def _():
-        f_in[...] = jnp.zeros(f_in.shape, jnp.float32)
-
-    @pl.when(last)
-    def _():
-        o_in[...] = jnp.zeros(o_in.shape, jnp.float32)
+    for j in range(2, N):
+
+        @pl.when(place >= j)
+        def _():
+            up_map(j - 1).wait_recv()
+
+        @pl.when(N - 1 - place >= j)
+        def _():
+            down_map(j - 1).wait_recv()
+
+        if j < N - 1:
+
+            @pl.when(sends_up(j))
+            def _():
+                put(up_out, j, mat_mat([end_map[c] for c in range(9)], planes(up_in, j - 1, 9)))
+                up_map(j).start()
+
+            @pl.when(sends_down(j))
+            def _():
+                put(
+                    down_out, j,
+                    mat_mat([maps[0, 9 + c] for c in range(9)], planes(down_in, j - 1, 9)),
+                )
+                down_map(j).start()
 
     total = [part[me, c] for c in range(4)]
     mask_up.wait_recv()
@@ -306,10 +344,14 @@
             to_surf(edge_out.at[sweep, 0], edge_in.at[sweep, 1], edge_send.at[sweep, 1], edge_recv.at[sweep, 1], before),
         ]
 
-    def chain_copies(sweep):
-        return (
-            to_norm(f_out.at[sweep], f_in.at[sweep], f_send.at[sweep], f_recv.at[sweep], place + 1),
-            to_norm(o_out.at[sweep], o_in.at[sweep], o_send.at[sweep], o_recv.at[sweep], place - 1),
+    def up_copy(sweep, j):
+        return to_norm(
+            f_out.at[sweep], f_in.at[sweep, j], f_send.at[sweep, j], f_recv.at[sweep, j], place + j
+        )
+
+    def down_copy(sweep, j):
+        return to_norm(
+            o_out.at[sweep], o_in.at[sweep, j], o_send.at[sweep, j], o_recv.at[sweep, j], place - j
         )
 
     for sweep in range(SWEEPS):
@@ -351,70 +393,56 @@
             return state
 
         tops = lax.fori_loop(1, K, backward, ends)
-        for c in range(3):
-            edge[0, c] = ends[c]
-            edge[1, c] = tops[c]
-
-        f_copy, o_copy = chain_copies(sweep)
-
-        def own(which):
-            return [edge[which, c] for c in range(3)]
-
-        def end_state(entering):
-            return added(own(0), mat_vec([end_map[c] for c in range(9)], entering))
-
-        def leaving(state):
-            return added(
-                planes(o_in, sweep), mat_vec([h_in[c] for c in range(9)], state)
-            )
-
-        @pl.when(place < half)
+        put(f_out, sweep, ends)
+        for j in range(N - 1, 0, -1):
+
+            @pl.when(place + j < N)
+            def _():
+                up_copy(sweep, j).start()
+
+        if sweep == 0:
+
+            @pl.when(first)
+            def _():
+                h_copy.wait_recv()
+
+        @pl.when(jnp.logical_not(first))
         def _():
-            @pl.when(jnp.logical_not(first))
-            def _():
-                f_copy.wait_recv()
-
-            entering = planes(f_in, sweep)
-            state = end_state(entering)
-            put(f_out, sweep, state)
-            f_copy.start()
-            o_copy.wait_recv()
-            above = leaving(state)
-            for c in range(3):
-                o_true[c] = above[c]
-
-            @pl.when(jnp.logical_not(first))
-            def _():
-                top = added(own(1), mat_vec([maps[0, c] for c in range(9)], entering))
-                top = added(top, mat_vec([maps[0, 9 + c] for c in range(9)], above))
-                put(o_out, sweep, top)
-                o_copy.start()
-
-        @pl.when(place >= half)
-        def _():
-            @pl.when(jnp.logical_not(last))
-            def _():
-                o_copy.wait_recv()
-
             top = added(
-                own(1), mat_vec([maps[0, 9 + c] for c in range(9)], leaving(own(0)))
+                tops,
+                mat_vec(
+                    [maps[0, 9 + c] for c in range(9)], mat_vec([h_in[c] for c in range(9)], ends)
+                ),
             )
             put(o_out, sweep, top)
-            o_copy.start()
-            f_copy.wait_recv()
-            state = end_state(planes(f_in, sweep))
-
-            @pl.when(jnp.logical_not(last))
-            def _():
-                put(f_out, sweep, state)
-                f_copy.start()
-
-            above = leaving(state)
-            for c in range(3):
-                o_true[c] = above[c]
-
-        entering = planes(f_in, sweep)
-        above = [o_true[c] for c in range(3)]
+            for j in range(N - 1, 0, -1):
+
+                @pl.when(place - j >= 0)
+                def _():
+                    down_copy(sweep, j).start()
+
+        enter[...] = jnp.zeros(enter.shape, jnp.float32)
+        for j in range(1, N):
+
+            @pl.when(place - j >= 0)
+            def _():
+                up_copy(sweep, j).wait_recv()
+                moved = planes(f_in.at[sweep], j)
+                if j > 1:
+                    moved = mat_vec(planes(up_in, j - 1, 9), moved)
+                put(enter, 0, added(planes(enter, 0), moved))
+
+            @pl.when(place + j < N)
+            def _():
+                down_copy(sweep, j).wait_recv()
+                moved = planes(o_in.at[sweep], j)
+                if j > 1:
+                    moved = mat_vec(planes(down_in, j - 1, 9), moved)
+                put(enter, 1, added(planes(enter, 1), moved))
+
+        entering = planes(enter, 0)
+        state = added(ends, mat_vec([end_map[c] for c in range(9)], entering))
+        above = added(planes(enter, 1), mat_vec([h_in[c] for c in range(9)], state))
 
         def finish(k, carry, sweep=sweep):
             state = added(planes(values, k), mat_vec(planes(maps, k, 9), entering))
@@ -441,27 +469,38 @@
         for copy in edge_copies(sweep):
             copy.wait_send()
 
-    @pl.when(place >= half)
-    def _():
-        h_copy.wait_send()
-
     @pl.when(jnp.logical_not(first))
     def _():
         link_copy.wait_send()
+        h_copy.wait_send()
+
+    for j in range(1, N):
+        if j < N - 1:
+
+            @pl.when(sends_up(j))
+            def _():
+                up_map(j).wait_send()
+
+            @pl.when(sends_down(j))
+            def _():
+                down_map(j).wait_send()
+
         for sweep in range(SWEEPS):
-            chain_copies(sweep)[1].wait_send()
-
-    @pl.when(jnp.logical_not(last))
-    def _():
-        for sweep in range(SWEEPS):
-            chain_copies(sweep)[0].wait_send()
+
+            @pl.when(place + j < N)
+            def _():
+                up_copy(sweep, j).wait_send()
+
+            @pl.when(place - j >= 0)
+            def _():
+                down_copy(sweep, j).wait_send()
 
 
 def per_device(
     surf_size, norm_size, mode_shapes, amplitude, mode_patch, column_patch, wall_mask, offsets,
     coupling, pivot_inv, stiffness,
 ):
-    S = surf_size
+    S, N = surf_size, norm_size
     modes = mode_shapes.transpose(0, 2, 1, 3)
     pivot = pivot_inv.transpose(0, 2, 1, 3)
     K, _, R, W = pivot.shape
@@ -493,13 +532,16 @@
             pltpu.VMEM((SWEEPS - 1, 2, 3, K, W), bf16),
             pltpu.VMEM((SWEEPS - 1, 2, 3, K, W), bf16),
             pltpu.VMEM((2, 3, K, W), f32),
+            pltpu.VMEM((SWEEPS, N, 3, R, W), f32),
             pltpu.VMEM((SWEEPS, 3, R, W), f32),
+            pltpu.VMEM((SWEEPS, N, 3, R, W), f32),
             pltpu.VMEM((SWEEPS, 3, R, W), f32),
-            pltpu.VMEM((SWEEPS, 3, R, W), f32),
-            pltpu.VMEM((SWEEPS, 3, R, W), f32),
-            pltpu.VMEM((3, R, W), f32),
             pltpu.VMEM((9, R, W), f32),
             pltpu.VMEM((9, R, W), f32),
+            pltpu.VMEM((N, 9, R, W), f32),
+            pltpu.VMEM((N, 9, R, W), f32),
+            pltpu.VMEM((N, 9, R, W), f32),
+            pltpu.VMEM((N, 9, R, W), f32),
             dma((3 + modes.shape[2] // (2 * R),)),
             dma((S,)),
             dma((S,)),
@@ -509,10 +551,14 @@
             dma,
             dma,
             dma,
-            dma((SWEEPS,)),
-            dma((SWEEPS,)),
-            dma((SWEEPS,)),
-            dma((SWEEPS,)),
+            dma((N,)),
+            dma((N,)),
+            dma((N,)),
+            dma((N,)),
+            dma((SWEEPS, N)),
+            dma((SWEEPS, N)),
+            dma((SWEEPS, N)),
+            dma((SWEEPS, N)),
             dma((SWEEPS - 1, 2)),
             dma((SWEEPS - 1, 2)),
         ],

time: 47.5 us -> 43.9 us (0.924)
  Pallas kernels: 45.5 us -> 41.9 us
    pallas_call x1, Pallas kernels: 45.5 us -> 41.9 us  [per_device(): pl.pallas_call(functools.partial(kernel, surf_size, norm_size), out_shape...]
where the time goes in v2:
time: 43.9 us; the launch traced here: 43.6 us
  Pallas kernels  41.9 us (95%)
  local copies, waits for them, and re-layouts  1.77 us (4%)
    pallas_call x1, Pallas kernels, per_device(): pl.pallas_call(functools.partial(kernel, surf_size, norm_size), out_shape...  41.9 us
    unnamed x1, local copies, waits for them, and re-layouts  1.77 us

profile of v2, /device:TPU:0, one launch (start us, length us, event | category | flops | bytes accessed | tf_op | source)
XLA Modules:
  0.0 43.6 jit_solution(15346208899753183833)
XLA Ops:
  0.0 41.9 %line_sweeps.1 = f32[16,3,8,256]{3,2,1,0:T(8,128)} custom-call(f32[128]{0:T(128)} %amplitude.1, s32[128]{0:T(128)} %mode_patch.1, s32[64,256]{1,0:T(8,128)} %column_patch.1, s32[8,256]{1,0:T(8,128)} %wall_mask.1, s32[8,256]{1,0:T(8,128)} %offsets.1, bf16[16,3,64,256]{3,2,1,0:T(8,128)(2,1)} %bitcast.3, f32[16,8,256]{2,1,0:T(8,128)} %coupling_hbm.1, ...), custom_call_target="tpu_custom_call" | custom-call | tf_op jit(solution)/shard_map/line_sweeps/pallas_call | solution.py:512
  41.9 1.8 %copy.11 = f32[16,8,3,256]{3,1,2,0:T(8,128)} copy(f32[16,8,3,256]{3,1,2,0:T(8,128)} %bitcast.4) | data formatting | bytes 786432

commit v3 on v2

--- a/solution.py
+++ b/solution.py
@@ -21,6 +21,10 @@
         return carry
 
     return lax.fori_loop(0, count // unroll, outer, init)
+
+
+def later(count, body, init, unroll=5):
+    return loop(count - 1, lambda step, carry: body(step + 1, carry), init, unroll)
 
 
 def mat_vec(matrix, vector):
@@ -382,7 +386,7 @@
             planes(pivot, 0, 9), added(source(0), [wall[c] for c in range(3)])
         )
         put(values, 0, start)
-        ends = lax.fori_loop(1, K, forward, start)
+        ends = later(K, forward, start)
 
         def backward(step, state):
             k = K - 1 - step
@@ -392,7 +396,7 @@
             put(values, k, state)
             return state
 
-        tops = lax.fori_loop(1, K, backward, ends)
+        tops = later(K, backward, ends)
         put(f_out, sweep, ends)
         for j in range(N - 1, 0, -1):
 
@@ -454,7 +458,7 @@
                     halo[1, c, pl.ds(k, 1), :] = state[c][R - 1 : R]
             return carry
 
-        loop(K, finish, 0, 2)
+        loop(K, finish, 0, 4)
         if sweep < SWEEPS - 1:
             for side in range(2):
                 edge_out[sweep, side] = halo[side].astype(jnp.bfloat16)

time: 43.9 us -> 41.7 us (0.950)
  Pallas kernels: 41.9 us -> 39.7 us
    pallas_call x1, Pallas kernels: 41.9 us -> 39.7 us  [per_device(): pl.pallas_call(functools.partial(kernel, surf_size, norm_size), out_shape...]
where the time goes in v3:
time: 41.7 us; the launch traced here: 41.5 us
  Pallas kernels  39.7 us (95%)
  local copies, waits for them, and re-layouts  1.77 us (4%)
    pallas_call x1, Pallas kernels, per_device(): pl.pallas_call(functools.partial(kernel, surf_size, norm_size), out_shape...  39.7 us
    unnamed x1, local copies, waits for them, and re-layouts  1.77 us

profile of v3, /device:TPU:0, one launch (start us, length us, event | category | flops | bytes accessed | tf_op | source)
XLA Modules:
  0.0 41.5 jit_solution(840929510857512643)
XLA Ops:
  0.0 39.7 %line_sweeps.1 = f32[16,3,8,256]{3,2,1,0:T(8,128)} custom-call(f32[128]{0:T(128)} %amplitude.1, s32[128]{0:T(128)} %mode_patch.1, s32[64,256]{1,0:T(8,128)} %column_patch.1, s32[8,256]{1,0:T(8,128)} %wall_mask.1, s32[8,256]{1,0:T(8,128)} %offsets.1, bf16[16,3,64,256]{3,2,1,0:T(8,128)(2,1)} %bitcast.3, f32[16,8,256]{2,1,0:T(8,128)} %coupling_hbm.1, ...), custom_call_target="tpu_custom_call" | custom-call | tf_op jit(solution)/shard_map/line_sweeps/pallas_call | solution.py:516
  39.7 1.8 %copy.11 = f32[16,8,3,256]{3,1,2,0:T(8,128)} copy(f32[16,8,3,256]{3,1,2,0:T(8,128)} %bitcast.4) | data formatting | bytes 786432
